TPU v7x, 128 devices: a whole 4x4x4 slice. The times are simulated.
128 devices in a mesh: gx: 8 (over z, core), gy: 16 (over y, x).
Axes of the slice: x: 4, y: 4, z: 4, core: 2. Of those that a mesh axis runs over, the one named last changes fastest.
Arguments:
- center_points: float32 [3, 8192], P(None, ('gx', 'gy')), may hold values from 0 to 1
- displacements: float32 [3, 8192], P(None, ('gx', 'gy')), may hold values from -24 to 24
- edge_points: float32 [3, 131072], P(None, ('gx', 'gy')), may hold values from 0 to 1
- send_list: int32 [128, 16, 3], P(('gx', 'gy')), may hold values from -1 to 15, as said below
- block_tiles: int32 [512, 12], P(('gx', 'gy')), may hold values from 0 to 47, as said below
- block_count: int32 [128], P(('gx', 'gy')), may hold values from 1 to 4, as said below
Outputs:
- coefficients: float32 [3, 8192], P(None, ('gx', 'gy'))
- block_motion: float32 [512, 3, 64, 4096], P(('gx', 'gy'))
Inputs may be any that keep to these rules, and one draw needn't show every extreme that they name: `send_list`: A zone is the 16 devices that share a gx index. Entry [s, r, c] names the local edge that device s sends to device r of its zone in position c, or -1 where that position carries nothing. Every position that a live block slot names carries an edge. `block_tiles`: the entry for a block slot and edge is the position s * 3 + c, in the tiles that reach the block's device, of the tile sent by device s of its zone in position c; the 48 entries of one device are all distinct, so a device with 4 live blocks receives 3 tiles from every device of its zone. `block_count`: the live slots of a device are its first ones; in every zone some device holds 4 blocks.
All inputs are finite; a program needn't handle non-finite values.
Results may differ from a plain program's by a relative error of at most 0.0003.
Values sent between devices are 32-bit elements; how exact they have to be, the bound alone decides.
A program may use at most 128 MiB of HBM per device.

v0:
```python
import math

import jax
import jax.numpy as jnp
from jax import lax
from jax.sharding import PartitionSpec as P

S = 64
ITERS = 3
SLOTS = 4
EDGE_DEV = 16


RADIUS = 0.25
SHIFT = 0.1
HIGHEST_PREC = lax.Precision.HIGHEST


def pair_distance(left_points, right_points):
    squared = (left_points[0][:, None] - right_points[0][None, :]) ** 2
    squared = squared + (left_points[1][:, None] - right_points[1][None, :]) ** 2
    squared = squared + (left_points[2][:, None] - right_points[2][None, :]) ** 2
    return squared


def wendland(squared):
    radial = jnp.sqrt(squared) / RADIUS
    remain = jnp.maximum(1.0 - radial, 0.0)
    return remain**4 * (4.0 * radial + 1.0)


def transfinite(edge_tiles):
    extent = edge_tiles.shape[2]
    fraction = jnp.arange(extent).astype(jnp.float32) / (extent - 1)
    blends = jnp.stack([1.0 - fraction, fraction])
    pair_weight = (blends[None, :, :, None] * blends[:, None, None, :]).reshape(4, extent, extent)
    first_dir = edge_tiles[:, 0:4]
    second_dir = edge_tiles[:, 4:8]
    third_dir = edge_tiles[:, 8:12]
    straight = (
        blends[0][None, None, :] * first_dir[:, :, 0:1]
        + blends[1][None, None, :] * first_dir[:, :, extent - 1 : extent]
    )
    result = jnp.einsum(
        "cei,ejk->cijk", first_dir - 2.0 * straight, pair_weight, precision=HIGHEST_PREC
    )
    result = result + jnp.einsum("cej,eik->cijk", second_dir, pair_weight, precision=HIGHEST_PREC)
    result = result + jnp.einsum("cek,eij->cijk", third_dir, pair_weight, precision=HIGHEST_PREC)
    return result.reshape(3, extent, extent * extent)


def conjugate(right_side, matvec, global_sum):
    norm_start = global_sum(jnp.sum(right_side * right_side, axis=1, keepdims=True))

    def cg_turn(iteration, cg_state):
        iterate, remain, search, norm_now = cg_state
        applied = matvec(search)
        step_size = norm_now / global_sum(jnp.sum(search * applied, axis=1, keepdims=True))
        iterate = iterate + step_size * search
        remain = remain - step_size * applied
        norm_next = global_sum(jnp.sum(remain * remain, axis=1, keepdims=True))
        search = remain + norm_next / norm_now * search
        return (iterate, remain, search, norm_next)

    cg_state = lax.fori_loop(
        0, ITERS, cg_turn, (jnp.zeros_like(right_side), right_side, right_side, norm_start)
    )
    return cg_state[0]


def row_product(full_search, kernel):
    return lax.dot_general(full_search, kernel, (((1,), (1,)), ((), ())), precision=HIGHEST_PREC)


def make_fold(points, all_centers, running, portion):
    extent = portion.shape[1]
    step_cols = math.gcd(extent, 2048)

    def add_block(number, summed):
        first_col = number * step_cols
        part_coef = lax.dynamic_slice_in_dim(portion, first_col, step_cols, 1)
        part_cent = lax.dynamic_slice_in_dim(all_centers, first_col, step_cols, 1)
        weights = wendland(pair_distance(points, part_cent))
        return summed + row_product(part_coef, weights)

    return lax.fori_loop(0, extent // step_cols, add_block, running)


def shards(center_points, displacements, edge_points, send_list, block_tiles, block_count):
    empty_motion = jnp.zeros((3, edge_points.shape[1]), jnp.float32)
    all_centers = lax.all_gather(center_points, ("gx", "gy"), axis=1, tiled=True)
    kernel = wendland(pair_distance(center_points, all_centers))

    def matvec(search):
        full_search = lax.all_gather(search, ("gx", "gy"), axis=1, tiled=True)
        return row_product(full_search, kernel) + SHIFT * search

    def global_sum(partial_value):
        return lax.psum(partial_value, ("gx", "gy"))

    coefficients = conjugate(displacements, matvec, global_sum)
    motion = make_fold(
        edge_points,
        all_centers,
        empty_motion,
        lax.all_gather(coefficients, ("gx", "gy"), axis=1, tiled=True),
    )
    group_size = lax.axis_size("gy")
    capacity = send_list.shape[2]
    motion_tiles = motion.reshape(3, EDGE_DEV, S)
    wanted = send_list[0].reshape(group_size * capacity)
    picked = jnp.take(motion_tiles, jnp.maximum(wanted, 0), axis=1)
    picked = jnp.where((wanted >= 0)[None, :, None], picked, 0.0)
    arrived = lax.all_to_all(
        picked.reshape(3, group_size * capacity * S), "gy", split_axis=1, concat_axis=1, tiled=True
    )
    arrived = arrived.reshape(3, group_size * capacity, S)
    live_blocks = block_count[0]

    def fill_block(position, result):
        edge_tiles = jnp.take(arrived, block_tiles[position], axis=1)
        return lax.dynamic_update_index_in_dim(result, transfinite(edge_tiles), position, 0)

    block_motion = lax.fori_loop(
        0, live_blocks, fill_block, jnp.zeros((SLOTS, 3, S, S * S), jnp.float32)
    )
    return (coefficients, block_motion)


def solution(mesh):
    return jax.shard_map(
        shards,
        mesh=mesh,
        in_specs=(
            P(None, ("gx", "gy")),
            P(None, ("gx", "gy")),
            P(None, ("gx", "gy")),
            P(("gx", "gy"), None, None),
            P(("gx", "gy"), None),
            P(("gx", "gy")),
        ),
        out_specs=(P(None, ("gx", "gy")), P(("gx", "gy"), None, None, None)),
        check_vma=False,
    )
```

profile of v0, /device:TPU:8, one launch (start us, length us, event | category | flops | bytes accessed | tf_op | source)
XLA Modules:
  0.0 1038.9 jit_solution(17612704965731299334)
XLA Ops:
  3.6 66.5 %psum.21 = f32[3,1]{0,1:T(1,128)S(1)} all-reduce(f32[3,1]{0,1:T(1,128)S(1)} %bitcast.160), channel_id=1, replica_groups=mesh['gx'=8,'gy'=16] {'gx','gy'}, use_global_device_ids=true, to_apply=%region_1.0 | all-reduce | flops 3 | bytes 24 | tf_op jit(solution)/shard_map/psum | solution.py:99
  70.9 59.2 %all-gather.1 = f32[128,64,3]{1,2,0:T(4,128)S(1)} all-gather(f32[1,64,3]{1,2,0:T(4,128)} %bitcast.159), channel_id=1, replica_groups=mesh['gx'=8,'gy'=16] {'gx','gy'}, dimensions={0}, use_global_device_ids=true | all-gather | bytes 99072 | tf_op jit(solution)/shard_map/all_gather | solution.py:91
  130.3 569.7 %while.44 = (s32[]{:T(128)}, f32[3,64]{1,0:T(4,128)S(1)}, f32[3,64]{1,0:T(4,128)S(1)}, f32[3,64]{1,0:T(4,128)S(1)}, f32[3,1]{0,1:T(1,128)S(1)}, /*index=5*/f32[8...) while((s32[]{:T(128)}, f32[3,64]{1,0:T(4,128)S(1)}, ...), condition=%wide.region_7.0_spmd.clone, body=%wide.region_2.0_spmd.clone.sunk | while | flops 27265480 | bytes 697683 | solution.py:65
  130.3 59.5 %all-gather.5 = f32[128,64,3]{1,2,0:T(4,128)S(1)} all-gather(f32[1,64,3]{1,2,0:T(4,128)S(1)} %bitcast.143), channel_id=1, replica_groups=mesh['gx'=8,'gy'=16] {'gx','gy'}, dimensions={0}, use_global_device_ids=true | all-gather | bytes 99072 | tf_op jit(solution)/shard_map/while/body/eval_jaxpr/all_gather | solution.py:95
  193.2 64.1 %psum.26 = f32[3,1]{0,1:T(1,128)S(1)} all-reduce(f32[3,1]{0,1:T(1,128)S(1)} %bitcast.161), channel_id=1, replica_groups=mesh['gx'=8,'gy'=16] {'gx','gy'}, use_global_device_ids=true, to_apply=%region_4.0 | all-reduce | flops 3 | bytes 24 | tf_op jit(solution)/shard_map/while/body/eval_jaxpr/psum | solution.py:99
  257.5 62.5 %psum.27 = f32[3,1]{0,1:T(1,128)S(1)} all-reduce(f32[3,1]{0,1:T(1,128)S(1)} %bitcast.156), channel_id=1, replica_groups=mesh['gx'=8,'gy'=16] {'gx','gy'}, use_global_device_ids=true, to_apply=%region_6.0 | all-reduce | flops 3 | bytes 24 | tf_op jit(solution)/shard_map/while/body/eval_jaxpr/psum | solution.py:99
  320.1 59.1 %all-gather.5 = f32[128,64,3]{1,2,0:T(4,128)S(1)} all-gather(f32[1,64,3]{1,2,0:T(4,128)S(1)} %bitcast.143), channel_id=1, replica_groups=mesh['gx'=8,'gy'=16] {'gx','gy'}, dimensions={0}, use_global_device_ids=true | all-gather | bytes 99072 | tf_op jit(solution)/shard_map/while/body/eval_jaxpr/all_gather | solution.py:95
  382.5 65.0 %psum.26 = f32[3,1]{0,1:T(1,128)S(1)} all-reduce(f32[3,1]{0,1:T(1,128)S(1)} %bitcast.161), channel_id=1, replica_groups=mesh['gx'=8,'gy'=16] {'gx','gy'}, use_global_device_ids=true, to_apply=%region_4.0 | all-reduce | flops 3 | bytes 24 | tf_op jit(solution)/shard_map/while/body/eval_jaxpr/psum | solution.py:99
  447.8 62.1 %psum.27 = f32[3,1]{0,1:T(1,128)S(1)} all-reduce(f32[3,1]{0,1:T(1,128)S(1)} %bitcast.156), channel_id=1, replica_groups=mesh['gx'=8,'gy'=16] {'gx','gy'}, use_global_device_ids=true, to_apply=%region_6.0 | all-reduce | flops 3 | bytes 24 | tf_op jit(solution)/shard_map/while/body/eval_jaxpr/psum | solution.py:99
  510.0 59.2 %all-gather.5 = f32[128,64,3]{1,2,0:T(4,128)S(1)} all-gather(f32[1,64,3]{1,2,0:T(4,128)S(1)} %bitcast.143), channel_id=1, replica_groups=mesh['gx'=8,'gy'=16] {'gx','gy'}, dimensions={0}, use_global_device_ids=true | all-gather | bytes 99072 | tf_op jit(solution)/shard_map/while/body/eval_jaxpr/all_gather | solution.py:95
  572.6 65.0 %psum.26 = f32[3,1]{0,1:T(1,128)S(1)} all-reduce(f32[3,1]{0,1:T(1,128)S(1)} %bitcast.161), channel_id=1, replica_groups=mesh['gx'=8,'gy'=16] {'gx','gy'}, use_global_device_ids=true, to_apply=%region_4.0 | all-reduce | flops 3 | bytes 24 | tf_op jit(solution)/shard_map/while/body/eval_jaxpr/psum | solution.py:99
  637.8 62.1 %psum.27 = f32[3,1]{0,1:T(1,128)S(1)} all-reduce(f32[3,1]{0,1:T(1,128)S(1)} %bitcast.156), channel_id=1, replica_groups=mesh['gx'=8,'gy'=16] {'gx','gy'}, use_global_device_ids=true, to_apply=%region_6.0 | all-reduce | flops 3 | bytes 24 | tf_op jit(solution)/shard_map/while/body/eval_jaxpr/psum | solution.py:99
  700.0 59.5 %all-gather.2 = f32[128,64,3]{1,2,0:T(4,128)S(1)} all-gather(f32[1,64,3]{1,2,0:T(4,128)S(1)} %bitcast.152), channel_id=1, replica_groups=mesh['gx'=8,'gy'=16] {'gx','gy'}, dimensions={0}, use_global_device_ids=true | all-gather | bytes 99072 | tf_op jit(solution)/shard_map/all_gather | solution.py:106
  759.7 50.6 %while.45 = (s32[]{:T(128)}, f32[3,1024]{1,0:T(4,128)S(1)}, f32[3,8192]{1,0:T(4,128)S(1)}, f32[3,1024]{1,0:T(4,128)S(1)}, f32[3,8192]{1,0:T(4,128)S(1)}, /*index...) while((s32[]{:T(128)}, f32[3,1024]{1,0:T(4,128)S(1)}, ...), condition=%wide.region_9.0_spmd.clone, body=%wide.region_8.0_spmd.clone.sunk | while | flops 109058056 | bytes 172245 | solution.py:86
  759.8 12.5 %fusion.127 = f32[3,1024]{1,0:T(4,128)S(1)} fusion(f32[2048]{0:T(1024)S(1)} %bitcast.146, f32[1024]{0:T(1024)S(1)} %bitcast.150, f32[2048]{0:T(1024)S(1)} %bitcast.145, f32[1024]{0:T(1024)S(1)} %bitcast.151, f32[2048]{0:T(1024)S(1)} %bitcast.144, f32[1024]{0:T(1024)S(1)} %bitcast.149, f32[3,8192]{1,0:T(4,128)S(1)} %get-tuple-element.571, ...), kind=kOutput, calls=%fused_computation.71.clone.1 | convolution fusion | flops 109058048 | bytes 98309 | tf_op jit(solution)/shard_map/while/body/eval_jaxpr/dot_general | solution.py:72
  772.5 12.5 %fusion.127 = f32[3,1024]{1,0:T(4,128)S(1)} fusion(f32[2048]{0:T(1024)S(1)} %bitcast.146, f32[1024]{0:T(1024)S(1)} %bitcast.150, f32[2048]{0:T(1024)S(1)} %bitcast.145, f32[1024]{0:T(1024)S(1)} %bitcast.151, f32[2048]{0:T(1024)S(1)} %bitcast.144, f32[1024]{0:T(1024)S(1)} %bitcast.149, f32[3,8192]{1,0:T(4,128)S(1)} %get-tuple-element.571, ...), kind=kOutput, calls=%fused_computation.71.clone.1 | convolution fusion | flops 109058048 | bytes 98309 | tf_op jit(solution)/shard_map/while/body/eval_jaxpr/dot_general | solution.py:72
  785.1 12.5 %fusion.127 = f32[3,1024]{1,0:T(4,128)S(1)} fusion(f32[2048]{0:T(1024)S(1)} %bitcast.146, f32[1024]{0:T(1024)S(1)} %bitcast.150, f32[2048]{0:T(1024)S(1)} %bitcast.145, f32[1024]{0:T(1024)S(1)} %bitcast.151, f32[2048]{0:T(1024)S(1)} %bitcast.144, f32[1024]{0:T(1024)S(1)} %bitcast.149, f32[3,8192]{1,0:T(4,128)S(1)} %get-tuple-element.571, ...), kind=kOutput, calls=%fused_computation.71.clone.1 | convolution fusion | flops 109058048 | bytes 98309 | tf_op jit(solution)/shard_map/while/body/eval_jaxpr/dot_general | solution.py:72
  797.8 12.5 %fusion.127 = f32[3,1024]{1,0:T(4,128)S(1)} fusion(f32[2048]{0:T(1024)S(1)} %bitcast.146, f32[1024]{0:T(1024)S(1)} %bitcast.150, f32[2048]{0:T(1024)S(1)} %bitcast.145, f32[1024]{0:T(1024)S(1)} %bitcast.151, f32[2048]{0:T(1024)S(1)} %bitcast.144, f32[1024]{0:T(1024)S(1)} %bitcast.149, f32[3,8192]{1,0:T(4,128)S(1)} %get-tuple-element.571, ...), kind=kOutput, calls=%fused_computation.71.clone.1 | convolution fusion | flops 109058048 | bytes 98309 | tf_op jit(solution)/shard_map/while/body/eval_jaxpr/dot_general | solution.py:72
  831.1 206.8 %while.43 = (s32[]{:T(128)}, f32[4,3,64,4096]{3,2,1,0:T(8,128)}, s32[]{:T(128)}, s32[4,12]{1,0:T(4,128)S(1)}, f32[3,48,64]{2,0,1:T(4,128)S(1)}, /*index=5*/s32[]{:T(128)}, s32[]{:T(128)}, s32[]{:T(128)}) while((s32[]{:T(128)}, f32[4,3,64,4096]{3,2,1,0:T(8,128)}, s32[]{:T(128)}, s32[4,12]{1,0:T(4,128)S(1)}, f32[3,48,64]{2,0,1:T(4,128)S(1)}, ...), condition=%wide.region_11.12_spmd, body=%wide.region_10.11_spmd.sunk | while | flops 114876016 | bytes 41366100 | solution.py:124
  843.8 7.1 fusion.121
  850.9 8.9 fusion.122
  859.8 7.7 copy.89
  867.5 10.4 %bitcast_add_fusion.3 = f32[3,64,64,64]{3,1,2,0:T(8,128)S(1)} fusion(f32[3,64,64,64]{3,1,2,0:T(8,128)} %fusion.121, f32[64,64,3,64]{1,0,3,2:T(8,128)} %copy.89, f32[4,64]{0,1:T(8,128)S(1)} %copy.87, f32[4,64]{1,0:T(4,128)S(1)} %bitcast.141, f32[3,12,64]{2,1,0:T(8,128)S(1)} %fusion.120), kind=kOutput, calls=%fused_computation.79.clone.1 | convolution fusion | flops 39337984 | bytes 9478144 | tf_op jit(solution)/shard_map/while/body/cek,eij->cijk/dot_general | solution.py:48
  899.7 8.9 fusion.122
  908.6 7.7 copy.89
  916.3 10.4 %bitcast_add_fusion.3 = f32[3,64,64,64]{3,1,2,0:T(8,128)S(1)} fusion(f32[3,64,64,64]{3,1,2,0:T(8,128)} %fusion.121, f32[64,64,3,64]{1,0,3,2:T(8,128)} %copy.89, f32[4,64]{0,1:T(8,128)S(1)} %copy.87, f32[4,64]{1,0:T(4,128)S(1)} %bitcast.141, f32[3,12,64]{2,1,0:T(8,128)S(1)} %fusion.120), kind=kOutput, calls=%fused_computation.79.clone.1 | convolution fusion | flops 39337984 | bytes 9478144 | tf_op jit(solution)/shard_map/while/body/cek,eij->cijk/dot_general | solution.py:48
  948.5 8.9 fusion.122
  957.4 7.7 copy.89
  965.1 10.4 %bitcast_add_fusion.3 = f32[3,64,64,64]{3,1,2,0:T(8,128)S(1)} fusion(f32[3,64,64,64]{3,1,2,0:T(8,128)} %fusion.121, f32[64,64,3,64]{1,0,3,2:T(8,128)} %copy.89, f32[4,64]{0,1:T(8,128)S(1)} %copy.87, f32[4,64]{1,0:T(4,128)S(1)} %bitcast.141, f32[3,12,64]{2,1,0:T(8,128)S(1)} %fusion.120), kind=kOutput, calls=%fused_computation.79.clone.1 | convolution fusion | flops 39337984 | bytes 9478144 | tf_op jit(solution)/shard_map/while/body/cek,eij->cijk/dot_general | solution.py:48
  997.3 8.9 fusion.122
  1006.2 7.7 copy.89
  1013.9 10.4 %bitcast_add_fusion.3 = f32[3,64,64,64]{3,1,2,0:T(8,128)S(1)} fusion(f32[3,64,64,64]{3,1,2,0:T(8,128)} %fusion.121, f32[64,64,3,64]{1,0,3,2:T(8,128)} %copy.89, f32[4,64]{0,1:T(8,128)S(1)} %copy.87, f32[4,64]{1,0:T(4,128)S(1)} %bitcast.141, f32[3,12,64]{2,1,0:T(8,128)S(1)} %fusion.120), kind=kOutput, calls=%fused_computation.79.clone.1 | convolution fusion | flops 39337984 | bytes 9478144 | tf_op jit(solution)/shard_map/while/body/cek,eij->cijk/dot_general | solution.py:48
  (144 shorter events, 112.8 us)
Async XLA Ops:
  130.3 629.3 %copy-start = (f32[3,1024]{1,0:T(4,128)S(1)}, f32[3,1024]{1,0:T(4,128)}, u32[]{:S(2)}) copy-start(f32[3,1024]{1,0:T(4,128)} %param.14) | copy-start | bytes 36868
  700.0 59.6 %copy-start.1 = (f32[3,64]{1,0:T(4,128)}, f32[3,64]{1,0:T(4,128)S(1)}, u32[]{:S(2)}) copy-start(f32[3,64]{1,0:T(4,128)S(1)} %get-tuple-element.192) | copy-start | bytes 2308
  811.8 12.8 %all-to-all-start = ((f32[3,16,192]{2,0,1:T(4,128)}), f32[3,16,192]{2,0,1:T(4,128)S(1)}, u32[]{:S(2)}, u32[]{:S(2)}) async-start(f32[3,16,192]{2,0,1:T(4,128)} %copy.69), calls=%async_computation | async-start | bytes 131072 | tf_op jit(solution)/shard_map/all_to_all | solution.py:114
  824.7 6.4 copy-start.2
where the time goes:
time: 1040 us
  blocking collectives  744 us (72%)
  matrix products  166 us (16%)
  local copies, waits for them, and re-layouts  96.5 us (9%)
  loops' own time  14.9 us (1%)
    psum x7, blocking collectives, global_sum(): return lax.psum(partial_value, ('gx', 'gy'))  448 us
    all_gather x3, blocking collectives, matvec(): full_search = lax.all_gather(search, ('gx', 'gy'), axis=1, tiled=True)  178 us
    dot_general x7, matrix products, row_product(): lax.dot_general(full_search, kernel, (((1,), (1,)), ((), ())), precision=...  59.6 us
    all_gather x1, blocking collectives, shards(): lax.all_gather(coefficients, ('gx', 'gy'), axis=1, tiled=True)  59.5 us
    all_gather x1, blocking collectives, shards(): lax.all_gather(center_points, ('gx', 'gy'), axis=1, tiled=True)  59.2 us
    dot_general x4, matrix products, transfinite(): jnp.einsum('cek,eij->cijk', third_dir, pair_weight, precision=HIGHEST_PREC)  41.7 us
    dot_general x4, matrix products, transfinite(): jnp.einsum('cej,eik->cijk', second_dir, pair_weight, precision=HIGHEST_PREC)  35.7 us
    dot_general x4, local copies, waits for them, and re-layouts, transfinite(): jnp.einsum('cej,eik->cijk', second_dir, pair_weight, precision=HIGHEST_PREC)  30.9 us
  transfers between devices with their start and end apart: 1, of which 1 were waited for; matrix products, arithmetic and copies ran while one was open for 0% of the time, Pallas kernels for 0%

commit v1 on v0

v1 whole, which is shorter than its diff:
```python
import jax
import jax.numpy as jnp
from jax import lax
from jax.experimental import pallas as pl
from jax.experimental.pallas import tpu as pltpu
from jax.sharding import PartitionSpec as P

MESH = pl.DeviceIdType.MESH
F32 = jnp.float32
BF16 = jnp.bfloat16

NC = 8192
S = 64
SLOTS = 4
EDGE_DEV = 16
CAP = 3
N_GX = 8
N_GY = 16
CHIPS = 64
POINTS = EDGE_DEV * S
SHIFT = 0.1
CHUNK = 256
NCHUNK = NC // CHUNK
RING = (0, 1, 2, 1)
OFFSETS = sorted(
    [(a, b, c) for a in range(4) for b in range(4) for c in range(4) if (a, b, c) != (0, 0, 0)],
    key=lambda o: -sum(RING[q] for q in o),
)


def dot_nn(left, right):
    return lax.dot_general(left, right, (((1,), (0,)), ((), ())), preferred_element_type=F32)


def dot_nt(left, right):
    return lax.dot_general(left, right, (((1,), (1,)), ((), ())), preferred_element_type=F32)


def bump(squared):
    squared = jnp.maximum(squared, 1e-30)
    root = squared * lax.rsqrt(squared)
    t = jnp.maximum(4.0 - root, 0.0)
    t2 = t * t
    return (t2 * t2) * (5.0 - t)


def halves(v):
    high = v.astype(BF16)
    return high, (v - high.astype(F32)).astype(BF16)


def parts(v):
    high = v.astype(BF16).astype(F32)
    rest = v - high
    mid = rest.astype(BF16).astype(F32)
    return high, mid, rest - mid


def rows8(shape):
    return lax.broadcasted_iota(jnp.int32, shape, 0)


def left_stack(x8):
    row = rows8(x8.shape)
    norm = jnp.sum(x8 * x8, axis=0, keepdims=True)
    v = jnp.where(row < 3, -2.0 * x8, jnp.where(row == 3, 1.0, jnp.where(row == 4, norm, 0.0)))
    h, m, l = parts(v)
    return jnp.concatenate([h, h, m, m, h, l, jnp.zeros_like(h), jnp.zeros_like(h)], axis=0)


def right_stack(x8):
    row = rows8(x8.shape)
    norm = jnp.sum(x8 * x8, axis=0, keepdims=True)
    v = jnp.where(row < 3, x8, jnp.where(row == 3, norm, jnp.where(row == 4, 1.0, 0.0)))
    h, m, l = parts(v)
    return jnp.concatenate([h, m, h, m, l, h, jnp.zeros_like(h), jnp.zeros_like(h)], axis=0)


def motion_kernel(
    cen_ref, dis_ref, pts_ref, list_ref, coef_ref, tile_ref,
    half, cbuf, g1, g2, g3, right, left, kh, kl, ph, plo, sf, sp,
    d_ref, x_ref, r_ref, s_ref, motion, outbox, inbox, p8, ssem, rsem,
):
    gx = lax.axis_index("gx")
    gy = lax.axis_index("gy")
    z = lax.div(gx, 2)
    core = lax.rem(gx, 2)
    y = lax.div(gy, 4)
    x = lax.rem(gy, 4)
    me = z * N_GY + gy

    barrier = pltpu.get_barrier_semaphore()
    for k in range(1, N_GY):
        pl.semaphore_signal(
            barrier, inc=1, device_id=(gx, lax.rem(gy + k, N_GY)), device_id_type=MESH
        )
    for k in range(1, N_GX):
        pl.semaphore_signal(
            barrier, inc=1, device_id=(lax.rem(gx + k, N_GX), gy), device_id_type=MESH
        )

    half[gx] = jnp.zeros((8, 128), F32)
    half[gx, 0:3, 0:S] = cen_ref[...]
    half[gx, 4:7, 0:S] = dis_ref[...]
    p8[...] = jnp.zeros((8, POINTS), F32)
    p8[0:3, :] = 16.0 * (pts_ref[...] - 0.5)
    sf[...] = jnp.zeros((16, NC), F32)
    for b in range(POINTS // 128):
        stack = left_stack(p8[:, b * 128 : (b + 1) * 128])
        left[b * 128 : (b + 1) * 128, :] = jnp.transpose(stack).astype(BF16)

    pl.semaphore_wait(barrier, N_GY - 1 + N_GX - 1)

    for k in range(1, N_GX):
        pltpu.make_async_remote_copy(
            src_ref=half.at[gx], dst_ref=half.at[gx], send_sem=ssem.at[0], recv_sem=rsem.at[0],
            device_id=(lax.rem(gx + k, N_GX), gy), device_id_type=MESH,
        ).start()
    seven = half.at[0 : N_GX - 1]
    pltpu.make_async_copy(seven, seven, rsem.at[0]).wait()
    lane = lax.broadcasted_iota(jnp.int32, (8, 128), 1)
    for zz in range(4):
        cbuf[zz, gy] = jnp.where(lane < S, half[2 * zz], pltpu.roll(half[2 * zz + 1], S, axis=1))
    for k in range(1, N_GY):
        pltpu.make_async_remote_copy(
            src_ref=cbuf.at[:, gy], dst_ref=cbuf.at[:, gy], send_sem=ssem.at[1], recv_sem=rsem.at[1],
            device_id=(gx, lax.rem(gy + k, N_GY)), device_id_type=MESH,
        ).start()

    own = cbuf[z, gy]
    own = jnp.where(rows8((8, 128)) < 3, 16.0 * (own - 0.5), 0.0)
    left[POINTS : POINTS + 128, :] = jnp.transpose(left_stack(own)).astype(BF16)
    fifteen = cbuf.at[:, 0 : N_GY - 1]
    pltpu.make_async_copy(fifteen, fifteen, rsem.at[1]).wait()

    def build(i, _):
        zz = lax.div(i, 2)
        g0 = lax.rem(i, 2) * 8
        cols = pl.ds(pl.multiple_of(i * 1024, 1024), 1024)
        t = jnp.concatenate([cbuf[zz, g0 + k] for k in range(8)], axis=1)
        x8 = jnp.where(rows8((8, 1024)) < 3, 16.0 * (t - 0.5), 0.0)
        right[:, cols] = right_stack(x8).astype(BF16)
        d_ref[:, cols] = jnp.concatenate([cbuf[zz, g0 + k, 4:8, :] for k in range(8)], axis=1)
        return 0

    lax.fori_loop(0, 8, build, 0)

    def fill_own(n, _):
        cols = pl.ds(pl.multiple_of(n * CHUNK, CHUNK), CHUNK)
        high, low = halves(bump(dot_nn(left[POINTS : POINTS + 128, :], right[:, cols])))
        kh[:, cols] = high
        kl[:, cols] = low
        return 0

    lax.fori_loop(0, NCHUNK, fill_own, 0)

    def fill_edges(n, _):
        cols = pl.ds(pl.multiple_of(n * CHUNK, CHUNK), CHUNK)
        for b in range(POINTS // 256):
            rows = slice(b * 256, (b + 1) * 256)
            high, low = halves(bump(dot_nn(left[rows, :], right[:, cols])))
            ph[rows, cols] = high
            plo[rows, cols] = low
        return 0

    def set_search(search):
        high = search.astype(BF16).astype(F32)
        sf[8:12, :] = high
        sf[12:16, :] = search - high

    def apply_own():
        sp[...] = sf[...].astype(BF16)
        product = dot_nt(kh[...], sp[...]) + dot_nt(kl[...], sp[...])
        t = jnp.transpose(product)
        return (t[8:12] + t[12:16]) * (1.0 / 256.0)

    def spread(buf, slot):
        for a, b, c in OFFSETS:
            zz = lax.rem(z + a, 4)
            to = (2 * zz + core, lax.rem(y + b, 4) * 4 + lax.rem(x + c, 4))
            pltpu.make_async_remote_copy(
                src_ref=buf.at[me], dst_ref=buf.at[me], send_sem=ssem.at[slot],
                recv_sem=rsem.at[slot], device_id=to, device_id_type=MESH,
            ).start()

    def arrive(buf, slot):
        rest = buf.at[0 : CHIPS - 1]
        pltpu.make_async_copy(rest, rest, rsem.at[slot]).wait()

    def collected(buf):
        return jnp.concatenate([buf[q] for q in range(CHIPS)], axis=1)

    def total(v):
        return jnp.sum(v, axis=1, keepdims=True)

    live = lax.broadcasted_iota(jnp.int32, (4, 1), 0) < 3

    def ratio(top, bottom):
        return top / jnp.where(live, bottom, 1.0)

    set_search(d_ref[...])
    g1[me] = apply_own()
    spread(g1, 2)
    lax.fori_loop(0, NCHUNK // 2, fill_edges, 0)
    arrive(g1, 2)
    d = d_ref[...]
    rr0 = total(d * d)
    applied = collected(g1) + SHIFT * d
    step = ratio(rr0, total(d * applied))
    remain = d - step * applied
    rr1 = total(remain * remain)
    search = remain + ratio(rr1, rr0) * d
    x_ref[...] = step * d
    r_ref[...] = remain
    s_ref[...] = search

    set_search(search)
    g2[me] = apply_own()
    spread(g2, 3)
    lax.fori_loop(NCHUNK // 2, NCHUNK, fill_edges, 0)
    arrive(g2, 3)
    search = s_ref[...]
    applied = collected(g2) + SHIFT * search
    step = ratio(rr1, total(search * applied))
    iterate = x_ref[...] + step * search
    remain = r_ref[...] - step * applied
    rr2 = total(remain * remain)
    search = remain + ratio(rr2, rr1) * search
    x_ref[...] = iterate
    s_ref[...] = search
    set_search(search)
    high = iterate.astype(BF16).astype(F32)
    sf[0:4, :] = high
    sf[4:8, :] = iterate - high

    mine = pl.ds(pl.multiple_of(me * 128, 128), 128)
    last = apply_own()
    own_search = s_ref[:, mine]
    g3[me] = own_search * (last + SHIFT * own_search)
    spread(g3, 4)

    lane4 = lax.broadcasted_iota(jnp.int32, (4, 128), 1) < S

    def evaluate(b, _):
        rows = pl.ds(pl.multiple_of(b * 128, 128), 128)
        t = jnp.transpose(dot_nt(ph[rows, :], sp[...]) + dot_nt(plo[rows, :], sp[...]))
        first = (t[0:4] + t[4:8]) * (1.0 / 256.0)
        second = (t[8:12] + t[12:16]) * (1.0 / 256.0)
        motion[2 * b] = jnp.where(lane4, first, pltpu.roll(second, S, axis=1))
        motion[2 * b + 1] = jnp.where(lane4, pltpu.roll(first, S, axis=1), second)
        return 0

    lax.fori_loop(0, POINTS // 128, evaluate, 0)

    for k in range(N_GY):
        to = lax.rem(gy + k, N_GY)
        for c in range(CAP):
            tile = motion[jnp.maximum(list_ref[to, c], 0)]
            if k == 0:
                inbox[gy, c] = tile
            else:
                outbox[k, c] = tile
    for k in range(1, N_GY):
        pltpu.make_async_remote_copy(
            src_ref=outbox.at[k], dst_ref=inbox.at[gy], send_sem=ssem.at[5], recv_sem=rsem.at[5],
            device_id=(gx, lax.rem(gy + k, N_GY)), device_id_type=MESH,
        ).start()

    arrive(g3, 4)
    summed = g3[0]
    for q in range(1, CHIPS):
        summed = summed + g3[q]
    step = ratio(rr2, total(summed))
    result = x_ref[:, mine] + step * s_ref[:, mine]
    result = jnp.where(core == 0, result, pltpu.roll(result, S, axis=1))
    coef_ref[...] = result[0:3, 0:S]

    box = inbox.at[0 : N_GY - 1]
    pltpu.make_async_copy(box, box, rsem.at[5]).wait()
    for s in range(N_GY):
        for c in range(CAP):
            tile = inbox[s, c]
            other = pltpu.roll(tile, S, axis=1)
            first = jnp.where(lane4, tile, other)
            second = jnp.where(lane4, other, tile)
            tile_ref[s * CAP + c] = first + step * second

    pltpu.make_async_copy(seven, seven, ssem.at[0]).wait()
    pltpu.make_async_copy(fifteen, fifteen, ssem.at[1]).wait()
    for buf, slot in ((g1, 2), (g2, 3), (g3, 4)):
        rest = buf.at[0 : CHIPS - 1]
        pltpu.make_async_copy(rest, rest, ssem.at[slot]).wait()
    pltpu.make_async_copy(box, box, ssem.at[5]).wait()


WIDTH = 512


def blend_kernel(table_ref, count_ref, tile_ref, out_ref, st, lhs):
    n = pl.program_id(0)

    @pl.when(n == 0)
    def _():
        for b in range(SLOTS):
            for e in range(12):
                st[e, 4 * b : 4 * b + 4, :] = tile_ref[table_ref[b, e]]
        lane = lax.broadcasted_iota(jnp.int32, (1, 128), 1)
        w1 = jnp.where(lane < S, lane, lane - S).astype(F32) / (S - 1)
        w0 = 1.0 - w1
        first = jnp.concatenate([st[e] for e in range(4)], axis=0)
        edge = first - 2.0 * (w0 * first[:, 0:1] + w1 * first[:, S - 1 : S])
        wide = jnp.concatenate(
            [edge, jnp.broadcast_to(w0, (16, 128)), jnp.broadcast_to(w1, (16, 128)),
             jnp.zeros((32, 128), F32)],
            axis=0,
        )
        base = jnp.transpose(wide)[0:S]
        high = base.astype(BF16).astype(F32)
        low = base - high
        col = lax.rem(lax.broadcasted_iota(jnp.int32, (S, 128), 1), 16)
        for b in range(SLOTS):
            alive = b < count_ref[0]
            for c in range(3):
                keep = jnp.logical_and(col == 4 * b + c, alive)
                kh = jnp.where(keep, high, 0.0).astype(BF16)
                rows = slice((b * 3 + c) * S, (b * 3 + c + 1) * S)
                lhs[rows, 0:128] = kh
                lhs[rows, 128:256] = kh
                lhs[rows, 256:384] = jnp.where(keep, low, 0.0).astype(BF16)

    spot = n * WIDTH + lax.broadcasted_iota(jnp.int32, (128, WIDTH), 1)
    pick = jnp.where(lax.shift_right_logical(spot, 6) == lax.broadcasted_iota(jnp.int32, (128, WIDTH), 0), 1.0, 0.0).astype(BF16)
    second = jnp.concatenate([st[e] for e in range(4, 8)], axis=0)
    h, m, l = parts(second)
    spread = dot_nn(jnp.concatenate([h, m, l], axis=0).astype(BF16), pick)
    spread = spread[0:64] + spread[64:128] + spread[128:192]
    flat = n * WIDTH + lax.broadcasted_iota(jnp.int32, (16, WIDTH), 1)
    j1 = lax.shift_right_logical(flat, 6).astype(F32) / (S - 1)
    k1 = jnp.bitwise_and(flat, 63).astype(F32) / (S - 1)
    j0 = 1.0 - j1
    k0 = 1.0 - k1
    third = [jnp.concatenate([st[e]] * (WIDTH // 128), axis=1) for e in range(8, 12)]
    h0 = spread[0:16] * k0 + spread[32:48] * k1 + third[0] * j0 + third[2] * j1
    h1 = spread[16:32] * k0 + spread[48:64] * k1 + third[1] * j0 + third[3] * j1
    rhs = jnp.concatenate(
        [j0 * k0, j1 * k0, j0 * k1, j1 * k1, h0, h1, jnp.zeros((32, WIDTH), F32)], axis=0
    )
    rh, rl = halves(rhs)
    full = dot_nn(lhs[...], jnp.concatenate([rh, rl, rh], axis=0))
    for b in range(SLOTS):
        for c in range(3):
            out_ref[b, c] = full[(b * 3 + c) * S : (b * 3 + c + 1) * S]


def shards(center_points, displacements, edge_points, send_list, block_tiles, block_count):
    vmem = pl.BlockSpec(memory_space=pltpu.VMEM)
    smem = pl.BlockSpec(memory_space=pltpu.SMEM)
    coefficients, tiles = pl.pallas_call(
        motion_kernel,
        out_shape=(
            jax.ShapeDtypeStruct((3, S), F32),
            jax.ShapeDtypeStruct((N_GY * CAP, 4, 128), F32),
        ),
        in_specs=[vmem, vmem, vmem, smem],
        out_specs=(vmem, vmem),
        scratch_shapes=[
            pltpu.VMEM((N_GX, 8, 128), F32),
            pltpu.VMEM((4, N_GY, 8, 128), F32),
            pltpu.VMEM((CHIPS, 4, 128), F32),
            pltpu.VMEM((CHIPS, 4, 128), F32),
            pltpu.VMEM((CHIPS, 4, 128), F32),
            pltpu.VMEM((64, NC), BF16),
            pltpu.VMEM((POINTS + 128, 64), BF16),
            pltpu.VMEM((128, NC), BF16),
            pltpu.VMEM((128, NC), BF16),
            pltpu.VMEM((POINTS, NC), BF16),
            pltpu.VMEM((POINTS, NC), BF16),
            pltpu.VMEM((16, NC), F32),
            pltpu.VMEM((16, NC), BF16),
            pltpu.VMEM((4, NC), F32),
            pltpu.VMEM((4, NC), F32),
            pltpu.VMEM((4, NC), F32),
            pltpu.VMEM((4, NC), F32),
            pltpu.VMEM((EDGE_DEV, 4, 128), F32),
            pltpu.VMEM((N_GY, CAP, 4, 128), F32),
            pltpu.VMEM((N_GY, CAP, 4, 128), F32),
            pltpu.VMEM((8, POINTS), F32),
            pltpu.SemaphoreType.DMA((6,)),
            pltpu.SemaphoreType.DMA((6,)),
        ],
        compiler_params=pltpu.CompilerParams(
            collective_id=0, has_side_effects=True, vmem_limit_bytes=60 * 1024 * 1024
        ),
        name="motion",
    )(center_points, displacements, edge_points, send_list[0])
    block_motion = pl.pallas_call(
        blend_kernel,
        grid=(S * S // WIDTH,),
        out_shape=jax.ShapeDtypeStruct((SLOTS, 3, S, S * S), F32),
        in_specs=[smem, smem, vmem],
        out_specs=pl.BlockSpec((SLOTS, 3, S, WIDTH), lambda n: (0, 0, 0, n)),
        scratch_shapes=[
            pltpu.VMEM((12, 16, 128), F32),
            pltpu.VMEM((SLOTS * 3 * S, 384), BF16),
        ],
        name="blend",
    )(block_tiles, block_count, tiles)
    return (coefficients, block_motion)


def solution(mesh):
    return jax.shard_map(
        shards,
        mesh=mesh,
        in_specs=(
            P(None, ("gx", "gy")),
            P(None, ("gx", "gy")),
            P(None, ("gx", "gy")),
            P(("gx", "gy"), None, None),
            P(("gx", "gy"), None),
            P(("gx", "gy")),
        ),
        out_specs=(P(None, ("gx", "gy")), P(("gx", "gy"), None, None, None)),
        check_vma=False,
    )
```

time: 1040 us -> 80.2 us (0.08)
  the two profiles are of different devices: /device:TPU:8 before, /device:TPU:0 now
where the time goes in v1:
time: 80.2 us; the launch traced here: 80 us
  Pallas kernels  76.8 us (96%)
  local copies, waits for them, and re-layouts  1.94 us (2%)
  between operations  1.29 us (2%)
    pallas_call x1, Pallas kernels, shards(): pl.pallas_call(motion_kernel, out_shape=(jax.ShapeDtypeStruct((3, S), F32...  67.1 us
    pallas_call x1, Pallas kernels, shards(): pl.pallas_call(blend_kernel, grid=(S * S // WIDTH,), out_shape=jax.ShapeD...  9.67 us

profile of v1, /device:TPU:0, one launch (start us, length us, event | category | flops | bytes accessed | tf_op | source)
XLA Modules:
  0.0 80.0 jit_solution(2457896334659993528)
XLA Ops:
  1.3 1.4 %copy.9 = s32[1,16,3]{2,1,0:T(8,128)} copy(s32[1,16,3]{1,0,2:T(1,128)} %param.9) | data formatting | bytes 384 | tf_op jit(solution)/shard_map/squeeze | solution.py:395
  2.6 67.1 %motion.1 = (f32[3,64]{1,0:T(4,128)}, f32[48,4,128]{2,1,0:T(4,128)}) custom-call(f32[3,64]{1,0:T(4,128)} %cen_ref.1, f32[3,64]{1,0:T(4,128)} %dis_ref.1, f32[3,1024]{1,0:T(4,128)} %pts_ref.1, s32[16,3]{1,0:T(8,128)} %bitcast.1), custom_call_target="tpu_custom_call" | custom-call | tf_op jit(solution)/shard_map/motion/pallas_call | solution.py:358
  69.7 0.0 copy-start
  69.8 9.7 %blend.1 = f32[4,3,64,4096]{3,2,1,0:T(8,128)} custom-call(s32[4,12]{1,0:T(4,128)} %table_ref.1, s32[1]{0:T(128)S(6)} %copy.11.count_ref, f32[48,4,128]{2,1,0:T(4,128)} %get-tuple-element.5.tile_ref), custom_call_target="tpu_custom_call" | custom-call | tf_op jit(solution)/shard_map/blend/pallas_call | solution.py:396
  79.4 0.0 copy-done
  79.4 0.6 copy.12
Async XLA Ops:
  69.7 9.7 %copy-start = (f32[3,64]{1,0:T(4,128)S(1)}, f32[3,64]{1,0:T(4,128)}, u32[]{:S(2)}) copy-start(f32[3,64]{1,0:T(4,128)} %get-tuple-element.8) | copy-start | bytes 2308

commit v2 on v1

v2 whole, which is shorter than its diff:
```python
import functools

import jax
import jax.numpy as jnp
from jax import lax
from jax.experimental import pallas as pl
from jax.experimental.pallas import tpu as pltpu
from jax.sharding import PartitionSpec as P

MESH = pl.DeviceIdType.MESH
F32 = jnp.float32
BF16 = jnp.bfloat16

NC = 8192
S = 64
SLOTS = 4
EDGE_DEV = 16
CAP = 3
N_GX = 8
N_GY = 16
CHIPS = 64
POINTS = EDGE_DEV * S
SHIFT = 0.1
CHUNK = 256
NCHUNK = NC // CHUNK
RING = (0, 1, 2, 1)
OFFSETS = sorted(
    [(a, b, c) for a in range(4) for b in range(4) for c in range(4) if (a, b, c) != (0, 0, 0)],
    key=lambda o: -sum(RING[q] for q in o),
)


def dot_nn(left, right):
    return lax.dot_general(left, right, (((1,), (0,)), ((), ())), preferred_element_type=F32)


def dot_nt(left, right):
    return lax.dot_general(left, right, (((1,), (1,)), ((), ())), preferred_element_type=F32)


def bump(squared):
    squared = jnp.maximum(squared, 1e-30)
    root = squared * lax.rsqrt(squared)
    t = jnp.maximum(4.0 - root, 0.0)
    t2 = t * t
    return (t2 * t2) * (5.0 - t)


def halves(v):
    high = v.astype(BF16)
    return high, (v - high.astype(F32)).astype(BF16)


def parts(v):
    high = v.astype(BF16).astype(F32)
    rest = v - high
    mid = rest.astype(BF16).astype(F32)
    return high, mid, rest - mid


def rows8(shape):
    return lax.broadcasted_iota(jnp.int32, shape, 0)


def left_stack(x8):
    row = rows8(x8.shape)
    norm = jnp.sum(x8 * x8, axis=0, keepdims=True)
    v = jnp.where(row < 3, -2.0 * x8, jnp.where(row == 3, 1.0, jnp.where(row == 4, norm, 0.0)))
    h, m, l = parts(v)
    return jnp.concatenate([h, h, m, m, h, l, jnp.zeros_like(h), jnp.zeros_like(h)], axis=0)


def right_stack(x8):
    row = rows8(x8.shape)
    norm = jnp.sum(x8 * x8, axis=0, keepdims=True)
    v = jnp.where(row < 3, x8, jnp.where(row == 3, norm, jnp.where(row == 4, 1.0, 0.0)))
    h, m, l = parts(v)
    return jnp.concatenate([h, m, h, m, l, h, jnp.zeros_like(h), jnp.zeros_like(h)], axis=0)


STORED = 20
EARLY = 2
FIRST = 9
PER = 3
TALL = 64
AHEAD = 2


def motion_kernel(
    cen_ref, dis_ref, pts_ref, list_ref, coef_ref, tile_ref,
    half, cpos, cdis, g1, g2, g3, cst, pst, ost, own_k, stored, fresh, acc, sf, sp, xs,
    d_ref, x_ref, r_ref, s_ref, motion, outbox, inbox, p8, ssem, rsem,
):
    gx = lax.axis_index("gx")
    gy = lax.axis_index("gy")
    z = lax.div(gx, 2)
    core = lax.rem(gx, 2)
    y = lax.div(gy, 4)
    x = lax.rem(gy, 4)
    me = gy * 4 + z

    barrier = pltpu.get_barrier_semaphore()
    for k in range(1, N_GY):
        pl.semaphore_signal(
            barrier, inc=1, device_id=(gx, lax.rem(gy + k, N_GY)), device_id_type=MESH
        )
    for k in range(1, N_GX):
        pl.semaphore_signal(
            barrier, inc=1, device_id=(lax.rem(gx + k, N_GX), gy), device_id_type=MESH
        )

    half[gx] = jnp.zeros((8, 128), F32)
    half[gx, 0:3, 0:S] = cen_ref[...]
    half[gx, 4:7, 0:S] = dis_ref[...]
    p8[...] = jnp.zeros((8, POINTS), F32)
    p8[0:3, :] = 16.0 * (pts_ref[...] - 0.5)
    sf[...] = jnp.zeros((16, NC), F32)
    xs[...] = jnp.zeros((8, 512), F32)
    for b in range(POINTS // 128):
        cols = slice(b * 128, (b + 1) * 128)
        pst[:, cols] = left_stack(p8[:, cols]).astype(BF16)
    acc[...] = jnp.zeros((16, POINTS), F32)
    fresh[...] = jnp.zeros((8, 4 * CHUNK, 128), BF16)

    pl.semaphore_wait(barrier, N_GY - 1 + N_GX - 1)

    for k in range(1, N_GX):
        pltpu.make_async_remote_copy(
            src_ref=half.at[gx], dst_ref=half.at[gx], send_sem=ssem.at[0], recv_sem=rsem.at[0],
            device_id=(lax.rem(gx + k, N_GX), gy), device_id_type=MESH,
        ).start()
    seven = half.at[0 : N_GX - 1]
    pltpu.make_async_copy(seven, seven, rsem.at[0]).wait()
    lane = lax.broadcasted_iota(jnp.int32, (8, 128), 1)
    for zz in range(4):
        both = jnp.where(lane < S, half[2 * zz], pltpu.roll(half[2 * zz + 1], S, axis=1))
        cpos[gy, zz] = both[0:4]
        cdis[gy, zz] = both[4:8]
    for buf, slot in ((cpos, 1), (cdis, 6)):
        for k in range(1, N_GY):
            pltpu.make_async_remote_copy(
                src_ref=buf.at[gy], dst_ref=buf.at[gy], send_sem=ssem.at[slot],
                recv_sem=rsem.at[slot], device_id=(gx, lax.rem(gy + k, N_GY)),
                device_id_type=MESH,
            ).start()

    def centred(t):
        return jnp.where(rows8(t.shape) < 3, 16.0 * (t - 0.5), 0.0)

    def build(k, _):
        line = lax.rem(gy + k, N_GY)
        rows = pl.ds(pl.multiple_of(k * 512, 512), 512)
        xs[0:4, :] = centred(jnp.concatenate([cpos[line, zz] for zz in range(4)], axis=1))
        cst[rows, :] = jnp.transpose(right_stack(xs[...])).astype(BF16)
        return 0

    def fill_own(n, _):
        rows = pl.ds(pl.multiple_of(n * CHUNK, CHUNK), CHUNK)
        base = pl.multiple_of(n * (2 * CHUNK), 2 * CHUNK)
        high, low = halves(bump(dot_nn(cst[rows, :], ost[...])))
        own_k[pl.ds(base, CHUNK), :] = high
        own_k[pl.ds(base + CHUNK, CHUNK), :] = low
        return 0

    def fill(dst, jobs, extras):
        blocks = [
            (n, base, jb, pp)
            for n, base in jobs
            for jb in range(CHUNK // TALL)
            for pp in range(POINTS // 256)
        ]

        def distance(block):
            n, _, jb, pp = block
            rows = pl.ds(pl.multiple_of(n * CHUNK + jb * TALL, TALL), TALL)
            return dot_nn(cst[rows, :], pst[:, pp * 256 : (pp + 1) * 256])

        ready = [distance(block) for block in blocks[:AHEAD]]
        for at, (n, base, jb, pp) in enumerate(blocks):
            if at + AHEAD < len(blocks):
                ready.append(distance(blocks[at + AHEAD]))
            for extra in extras.get(at, ()):
                extra()
            high, low = halves(bump(ready.pop(0)))
            for half_at in range(2):
                part = slice(half_at * 128, half_at * 128 + 128)
                dst[2 * pp + half_at, pl.ds(base + jb * TALL, TALL), :] = high[:, part]
                dst[2 * pp + half_at, pl.ds(base + CHUNK + jb * TALL, TALL), :] = low[:, part]

    def fill_edges(n, _):
        fill(stored, [(n, pl.multiple_of(n * (2 * CHUNK), 2 * CHUNK))], {})
        return 0

    build(0, 0)
    p8[:, 0:128] = jnp.zeros((8, 128), F32)
    p8[0:4, 0:128] = centred(cpos[gy, z])
    ost[...] = left_stack(p8[:, 0:128]).astype(BF16)
    lax.fori_loop(0, EARLY, fill_own, 0)
    lax.fori_loop(0, EARLY, fill_edges, 0)

    fifteen = cpos.at[0 : N_GY - 1]
    pltpu.make_async_copy(fifteen, fifteen, rsem.at[1]).wait()
    lax.fori_loop(1, N_GY, build, 0)
    lax.fori_loop(EARLY, NCHUNK, fill_own, 0, unroll=2)
    others = cdis.at[0 : N_GY - 1]
    pltpu.make_async_copy(others, others, rsem.at[6]).wait()
    order = [(lax.rem(gy + k, N_GY), zz) for k in range(N_GY) for zz in range(4)]
    d_ref[...] = jnp.concatenate([cdis[line, zz] for line, zz in order], axis=1)

    def set_search(search):
        high = search.astype(BF16).astype(F32)
        sf[8:12, :] = high
        sf[12:16, :] = search - high

    def apply_own():
        for n in range(NCHUNK):
            value = sf[:, n * CHUNK : (n + 1) * CHUNK].astype(BF16)
            sp[:, 2 * n * CHUNK : (2 * n + 1) * CHUNK] = value
            sp[:, (2 * n + 1) * CHUNK : (2 * n + 2) * CHUNK] = value
        t = dot_nn(sp[...], own_k[...])
        return (t[8:12] + t[12:16]) * (1.0 / 256.0)

    def spread(buf, slot):
        for a, b, c in OFFSETS:
            zz = lax.rem(z + a, 4)
            to = (2 * zz + core, lax.rem(y + b, 4) * 4 + lax.rem(x + c, 4))
            pltpu.make_async_remote_copy(
                src_ref=buf.at[me], dst_ref=buf.at[me], send_sem=ssem.at[slot],
                recv_sem=rsem.at[slot], device_id=to, device_id_type=MESH,
            ).start()

    def arrive(buf, slot):
        rest = buf.at[0 : CHIPS - 1]
        pltpu.make_async_copy(rest, rest, rsem.at[slot]).wait()

    def collected(buf):
        return jnp.concatenate([buf[line * 4 + zz] for line, zz in order], axis=1)

    def total(v):
        return jnp.sum(v, axis=1, keepdims=True)

    live = lax.broadcasted_iota(jnp.int32, (4, 1), 0) < 3

    def ratio(top, bottom):
        return top / jnp.where(live, bottom, 1.0)

    set_search(d_ref[...])
    g1[me] = apply_own()
    spread(g1, 2)
    lax.fori_loop(EARLY, EARLY + FIRST, fill_edges, 0)
    arrive(g1, 2)
    d = d_ref[...]
    rr0 = total(d * d)
    applied = collected(g1) + SHIFT * d
    step = ratio(rr0, total(d * applied))
    remain = d - step * applied
    rr1 = total(remain * remain)
    search = remain + ratio(rr1, rr0) * d
    x_ref[...] = step * d
    r_ref[...] = remain
    s_ref[...] = search

    set_search(search)
    g2[me] = apply_own()
    spread(g2, 3)
    lax.fori_loop(EARLY + FIRST, STORED, fill_edges, 0)
    arrive(g2, 3)
    search = s_ref[...]
    applied = collected(g2) + SHIFT * search
    step = ratio(rr1, total(search * applied))
    iterate = x_ref[...] + step * search
    remain = r_ref[...] - step * applied
    rr2 = total(remain * remain)
    search = remain + ratio(rr2, rr1) * search
    x_ref[...] = iterate
    s_ref[...] = search
    set_search(search)
    high = iterate.astype(BF16).astype(F32)
    sf[0:4, :] = high
    sf[4:8, :] = iterate - high

    mine = pl.ds(pl.multiple_of(z * 128, 128), 128)
    last = apply_own()
    own_search = s_ref[:, mine]
    g3[me] = own_search * (last + SHIFT * own_search)
    spread(g3, 4)

    lane4 = lax.broadcasted_iota(jnp.int32, (4, 128), 1) < S

    def contract(src, n, base, pp):
        lhs = sp[:, pl.ds(pl.multiple_of(n * (2 * CHUNK), 2 * CHUNK), 2 * CHUNK)]
        rows = pl.ds(base, 2 * CHUNK)
        cols = slice(pp * 256, (pp + 1) * 256)
        rhs = jnp.concatenate([src[2 * pp, rows, :], src[2 * pp + 1, rows, :]], axis=1)
        acc[:, cols] += dot_nn(lhs, rhs)

    def held(n, pp):
        contract(stored, n, pl.multiple_of(n * (2 * CHUNK), 2 * CHUNK), pp)

    def fused(i, _):
        now = STORED + 2 * i
        across = POINTS // 256
        blocks = 2 * (CHUNK // TALL) * across
        extras = {}
        for c in range(2):
            for pp in range(across):
                at = c * (blocks // 2) + pp
                extras.setdefault(at, []).append(
                    functools.partial(contract, fresh, now - 2 + c, c * 2 * CHUNK, pp)
                )
        places = [at for at in range(blocks) if at % (blocks // 2) >= across]
        pieces = [(n, pp) for n in range(PER) for pp in range(across)]
        for k, (n, pp) in enumerate(pieces):
            at = places[k * len(places) // len(pieces)]
            extras.setdefault(at, []).append(functools.partial(held, PER * i + n, pp))
        fill(fresh, [(now, 0), (now + 1, 2 * CHUNK)], extras)
        return 0

    turns = (NCHUNK - STORED) // 2
    lax.fori_loop(0, turns, fused, 0)
    for pp in range(POINTS // 256):
        for c in range(2):
            contract(fresh, NCHUNK - 2 + c, c * 2 * CHUNK, pp)
        for n in range(PER * turns, STORED):
            held(n, pp)

    for b in range(POINTS // 128):
        t = acc[:, b * 128 : (b + 1) * 128]
        first = (t[0:4] + t[4:8]) * (1.0 / 256.0)
        second = (t[8:12] + t[12:16]) * (1.0 / 256.0)
        motion[2 * b] = jnp.where(lane4, first, pltpu.roll(second, S, axis=1))
        motion[2 * b + 1] = jnp.where(lane4, pltpu.roll(first, S, axis=1), second)

    for k in range(N_GY):
        to = lax.rem(gy + k, N_GY)
        for c in range(CAP):
            tile = motion[jnp.maximum(list_ref[c, 0, to], 0)]
            if k == 0:
                inbox[gy, c] = tile
            else:
                outbox[k, c] = tile
    for k in range(1, N_GY):
        pltpu.make_async_remote_copy(
            src_ref=outbox.at[k], dst_ref=inbox.at[gy], send_sem=ssem.at[5], recv_sem=rsem.at[5],
            device_id=(gx, lax.rem(gy + k, N_GY)), device_id_type=MESH,
        ).start()

    arrive(g3, 4)
    summed = g3[0]
    for q in range(1, CHIPS):
        summed = summed + g3[q]
    step = ratio(rr2, total(summed))
    result = x_ref[:, mine] + step * s_ref[:, mine]
    result = jnp.where(core == 0, result, pltpu.roll(result, S, axis=1))
    coef_ref[...] = result[0:3, 0:S]

    pltpu.make_async_copy(seven, seven, ssem.at[0]).wait()
    pltpu.make_async_copy(fifteen, fifteen, ssem.at[1]).wait()
    pltpu.make_async_copy(others, others, ssem.at[6]).wait()
    for buf, slot in ((g1, 2), (g2, 3), (g3, 4)):
        rest = buf.at[0 : CHIPS - 1]
        pltpu.make_async_copy(rest, rest, ssem.at[slot]).wait()

    box = inbox.at[0 : N_GY - 1]
    pltpu.make_async_copy(box, box, rsem.at[5]).wait()
    for s in range(N_GY):
        for c in range(CAP):
            tile = inbox[s, c]
            other = pltpu.roll(tile, S, axis=1)
            first = jnp.where(lane4, tile, other)
            second = jnp.where(lane4, other, tile)
            tile_ref[s * CAP + c] = first + step * second
    pltpu.make_async_copy(box, box, ssem.at[5]).wait()


WIDTH = 512


def blend_kernel(table_ref, count_ref, tile_ref, coef_ref, out_ref, copy_ref, st, lhs):
    n = pl.program_id(0)

    @pl.when(n == 0)
    def _():
        copy_ref[...] = coef_ref[...]
        for b in range(SLOTS):
            for e in range(12):
                row = e * 12 + 3 * b
                st[row : row + 3, :] = tile_ref[table_ref[b, e]][0:3]
        lane = lax.broadcasted_iota(jnp.int32, (1, 128), 1)
        w1 = jnp.where(lane < S, lane, lane - S).astype(F32) / (S - 1)
        w0 = 1.0 - w1
        first = st[0:48, :]
        edge = first - 2.0 * (w0 * first[:, 0:1] + w1 * first[:, S - 1 : S])
        ramps = jnp.where(rows8((24, 128)) < 12, w0, w1)
        wide = jnp.concatenate([edge, ramps, jnp.zeros((8, 128), F32)], axis=0)
        high = wide.astype(BF16).astype(F32)
        stack = jnp.concatenate([high, high, wide - high, jnp.zeros((16, 128), F32)], axis=0)
        base = jnp.transpose(stack)[0:S]
        col = lax.rem(lax.rem(lax.broadcasted_iota(jnp.int32, (S, 256), 1), 80), 12)
        for b in range(SLOTS):
            alive = b < count_ref[0]
            for c in range(3):
                slot = 3 * b + c
                keep = jnp.logical_and(col == slot, alive)
                lhs[slot * S : (slot + 1) * S, :] = jnp.where(keep, base, 0.0).astype(BF16)

    spot = n * WIDTH + lax.broadcasted_iota(jnp.int32, (128, WIDTH), 1)
    cell = lax.broadcasted_iota(jnp.int32, (128, WIDTH), 0)
    pick = jnp.where(lax.shift_right_logical(spot, 6) == cell, 1.0, 0.0).astype(BF16)
    h, m, l = parts(st[48:96, :])
    spread = dot_nn(jnp.concatenate([h, m, l], axis=0).astype(BF16), pick)
    spread = spread[0:48] + spread[48:96] + spread[96:144]
    flat = n * WIDTH + lax.broadcasted_iota(jnp.int32, (8, WIDTH), 1)[0:1]
    j1 = lax.shift_right_logical(flat, 6).astype(F32) / (S - 1)
    k1 = jnp.bitwise_and(flat, 63).astype(F32) / (S - 1)
    j0 = 1.0 - j1
    k0 = 1.0 - k1
    third = jnp.concatenate([st[96:144, :]] * (WIDTH // 128), axis=1)
    sides = spread[0:24] * k0 + spread[24:48] * k1 + third[0:24] * j0 + third[24:48] * j1
    group = rows8((48, WIDTH))
    odd = jnp.logical_or(
        jnp.logical_and(group >= 12, group < 24), group >= 36
    )
    corner = jnp.where(odd, j1, j0) * jnp.where(group < 24, k0, k1)
    rh, rl = halves(jnp.concatenate([corner, sides, jnp.zeros((8, WIDTH), F32)], axis=0))
    rhs = jnp.concatenate([rh, rl, rh, jnp.zeros((16, WIDTH), BF16)], axis=0)
    full = dot_nn(lhs[...], rhs)
    for b in range(SLOTS):
        for c in range(3):
            out_ref[b, c] = full[(b * 3 + c) * S : (b * 3 + c + 1) * S]


def shards(center_points, displacements, edge_points, send_list, block_tiles, block_count):
    vmem = pl.BlockSpec(memory_space=pltpu.VMEM)
    smem = pl.BlockSpec(memory_space=pltpu.SMEM)
    coefficients, tiles = pl.pallas_call(
        motion_kernel,
        out_shape=(
            jax.ShapeDtypeStruct((3, S), F32),
            jax.ShapeDtypeStruct((N_GY * CAP, 4, 128), F32),
        ),
        in_specs=[vmem, vmem, vmem, smem],
        out_specs=(vmem, vmem),
        scratch_shapes=[
            pltpu.VMEM((N_GX, 8, 128), F32),
            pltpu.VMEM((N_GY, 4, 4, 128), F32),
            pltpu.VMEM((N_GY, 4, 4, 128), F32),
            pltpu.VMEM((CHIPS, 4, 128), F32),
            pltpu.VMEM((CHIPS, 4, 128), F32),
            pltpu.VMEM((CHIPS, 4, 128), F32),
            pltpu.VMEM((NC, 64), BF16),
            pltpu.VMEM((64, POINTS), BF16),
            pltpu.VMEM((64, 128), BF16),
            pltpu.VMEM((2 * NC, 128), BF16),
            pltpu.VMEM((POINTS // 128, STORED * 2 * CHUNK, 128), BF16),
            pltpu.VMEM((POINTS // 128, 4 * CHUNK, 128), BF16),
            pltpu.VMEM((16, POINTS), F32),
            pltpu.VMEM((16, NC), F32),
            pltpu.VMEM((16, 2 * NC), BF16),
            pltpu.VMEM((8, 512), F32),
            pltpu.VMEM((4, NC), F32),
            pltpu.VMEM((4, NC), F32),
            pltpu.VMEM((4, NC), F32),
            pltpu.VMEM((4, NC), F32),
            pltpu.VMEM((EDGE_DEV, 4, 128), F32),
            pltpu.VMEM((N_GY, CAP, 4, 128), F32),
            pltpu.VMEM((N_GY, CAP, 4, 128), F32),
            pltpu.VMEM((8, POINTS), F32),
            pltpu.SemaphoreType.DMA((7,)),
            pltpu.SemaphoreType.DMA((7,)),
        ],
        compiler_params=pltpu.CompilerParams(
            collective_id=0, has_side_effects=True, vmem_limit_bytes=60 * 1024 * 1024
        ),
        name="motion",
    )(center_points, displacements, edge_points, send_list.transpose(2, 0, 1))
    block_motion, coefficients = pl.pallas_call(
        blend_kernel,
        grid=(S * S // WIDTH,),
        out_shape=(
            jax.ShapeDtypeStruct((SLOTS, 3, S, S * S), F32),
            jax.ShapeDtypeStruct((3, S), F32),
        ),
        in_specs=[smem, smem, vmem, pl.BlockSpec((3, S), lambda n: (0, 0))],
        out_specs=(
            pl.BlockSpec((SLOTS, 3, S, WIDTH), lambda n: (0, 0, 0, n)),
            pl.BlockSpec((3, S), lambda n: (0, 0)),
        ),
        scratch_shapes=[
            pltpu.VMEM((144, 128), F32),
            pltpu.VMEM((SLOTS * 3 * S, 256), BF16),
        ],
        name="blend",
    )(block_tiles, block_count, tiles, coefficients)
    return (coefficients, block_motion)


def solution(mesh):
    return jax.shard_map(
        shards,
        mesh=mesh,
        in_specs=(
            P(None, ("gx", "gy")),
            P(None, ("gx", "gy")),
            P(None, ("gx", "gy")),
            P(("gx", "gy"), None, None),
            P(("gx", "gy"), None),
            P(("gx", "gy")),
        ),
        out_specs=(P(None, ("gx", "gy")), P(("gx", "gy"), None, None, None)),
        check_vma=False,
    )
```

time: 80.2 us -> 62.4 us (0.78)
  Pallas kernels: 76.8 us -> 60.9 us
  local copies, waits for them, and re-layouts: 1.94 us -> 0 us
    pallas_call x1, Pallas kernels: 67.1 us -> 52.4 us  [shards(): pl.pallas_call(motion_kernel, out_shape=(jax.ShapeDtypeStruct((3, S), F32...]
    squeeze x1 -> x0, local copies, waits for them, and re-layouts: 1.36 us -> none  [shards(): send_list[0]]
    pallas_call x1, Pallas kernels: 9.67 us -> 8.52 us  [shards(): pl.pallas_call(blend_kernel, grid=(S * S // WIDTH,), out_shape=(jax.Shape...]
where the time goes in v2:
time: 62.4 us; the launch traced here: 62.2 us
  Pallas kernels  60.9 us (98%)
  between operations  1.29 us (2%)
    pallas_call x1, Pallas kernels, shards(): pl.pallas_call(motion_kernel, out_shape=(jax.ShapeDtypeStruct((3, S), F32...  52.4 us
    pallas_call x1, Pallas kernels, shards(): pl.pallas_call(blend_kernel, grid=(S * S // WIDTH,), out_shape=(jax.Shape...  8.52 us

profile of v2, /device:TPU:0, one launch (start us, length us, event | category | flops | bytes accessed | tf_op | source)
XLA Modules:
  0.0 62.2 jit_solution(11955264446542302497)
XLA Ops:
  1.3 52.4 %motion.1 = (f32[3,64]{1,0:T(4,128)}, f32[48,4,128]{2,1,0:T(4,128)}) custom-call(f32[3,64]{1,0:T(4,128)} %cen_ref.1, f32[3,64]{1,0:T(4,128)} %dis_ref.1, f32[3,1024]{1,0:T(4,128)} %pts_ref.1, s32[3,1,16]{2,1,0:T(1,128)} %bitcast.1), custom_call_target="tpu_custom_call" | custom-call | tf_op jit(solution)/shard_map/motion/pallas_call | solution.py:436
  53.6 8.5 %blend.1 = (f32[4,3,64,4096]{3,2,1,0:T(8,128)}, f32[3,64]{1,0:T(4,128)}) custom-call(s32[4,12]{1,0:T(4,128)} %table_ref.1, s32[1]{0:T(128)S(6)} %copy.8.count_ref, f32[48,4,128]{2,1,0:T(4,128)} %get-tuple-element.6.tile_ref, f32[3,64]{1,0:T(4,128)} %get-tuple-element.7.coef_ref), custom_call_target="tpu_custom_call" | custom-call | tf_op jit(solution)/shard_map/blend/pallas_call | solution.py:477

commit v3 on v2

--- a/solution.py
+++ b/solution.py
@@ -24,10 +24,6 @@
 CHUNK = 256
 NCHUNK = NC // CHUNK
 RING = (0, 1, 2, 1)
-OFFSETS = sorted(
-    [(a, b, c) for a in range(4) for b in range(4) for c in range(4) if (a, b, c) != (0, 0, 0)],
-    key=lambda o: -sum(RING[q] for q in o),
-)
 
 
 def dot_nn(left, right):
@@ -78,12 +74,18 @@
     return jnp.concatenate([h, m, h, m, l, h, jnp.zeros_like(h), jnp.zeros_like(h)], axis=0)
 
 
-STORED = 20
-EARLY = 2
-FIRST = 9
-PER = 3
+EARLY = 6
+FIRST = 10
+GROUP = 2
+STORED = EARLY + 2 * FIRST
 TALL = 64
 AHEAD = 2
+OFFSETS = sorted(
+    [(a, b, c) for a in range(4) for b in range(4) for c in range(4) if (a, b, c) != (0, 0, 0)],
+    key=lambda o: -sum(RING[q] for q in o),
+)
+LINES = sorted(((a, b) for a in range(4) for b in range(4)), key=lambda o: RING[o[0]] + RING[o[1]])
+NEAR = 5
 
 
 def motion_kernel(
@@ -98,11 +100,12 @@
     y = lax.div(gy, 4)
     x = lax.rem(gy, 4)
     me = gy * 4 + z
+    lines = [lax.rem(y + a, 4) * 4 + lax.rem(x + b, 4) for a, b in LINES]
 
     barrier = pltpu.get_barrier_semaphore()
     for k in range(1, N_GY):
         pl.semaphore_signal(
-            barrier, inc=1, device_id=(gx, lax.rem(gy + k, N_GY)), device_id_type=MESH
+            barrier, inc=1, device_id=(gx, lines[k]), device_id_type=MESH
         )
     for k in range(1, N_GX):
         pl.semaphore_signal(
@@ -115,7 +118,7 @@
     p8[...] = jnp.zeros((8, POINTS), F32)
     p8[0:3, :] = 16.0 * (pts_ref[...] - 0.5)
     sf[...] = jnp.zeros((16, NC), F32)
-    xs[...] = jnp.zeros((8, 512), F32)
+    xs[...] = jnp.zeros((4, 8, 512), F32)
     for b in range(POINTS // 128):
         cols = slice(b * 128, (b + 1) * 128)
         pst[:, cols] = left_stack(p8[:, cols]).astype(BF16)
@@ -136,23 +139,25 @@
         both = jnp.where(lane < S, half[2 * zz], pltpu.roll(half[2 * zz + 1], S, axis=1))
         cpos[gy, zz] = both[0:4]
         cdis[gy, zz] = both[4:8]
-    for buf, slot in ((cpos, 1), (cdis, 6)):
+    def to_plane(src, dst, slot, far):
         for k in range(1, N_GY):
             pltpu.make_async_remote_copy(
-                src_ref=buf.at[gy], dst_ref=buf.at[gy], send_sem=ssem.at[slot],
-                recv_sem=rsem.at[slot], device_id=(gx, lax.rem(gy + k, N_GY)),
+                src_ref=src, dst_ref=dst, send_sem=ssem.at[slot],
+                recv_sem=rsem.at[slot if k < NEAR else far], device_id=(gx, lines[k]),
                 device_id_type=MESH,
             ).start()
 
+    to_plane(cpos.at[gy], cpos.at[gy], 1, 7)
+    to_plane(cdis.at[gy], cdis.at[gy], 6, 6)
+
     def centred(t):
         return jnp.where(rows8(t.shape) < 3, 16.0 * (t - 0.5), 0.0)
 
-    def build(k, _):
-        line = lax.rem(gy + k, N_GY)
-        rows = pl.ds(pl.multiple_of(k * 512, 512), 512)
-        xs[0:4, :] = centred(jnp.concatenate([cpos[line, zz] for zz in range(4)], axis=1))
-        cst[rows, :] = jnp.transpose(right_stack(xs[...])).astype(BF16)
-        return 0
+    def build(k):
+        line = lines[k]
+        rows = slice(k * 512, k * 512 + 512)
+        xs[k % 4, 0:4, :] = centred(jnp.concatenate([cpos[line, zz] for zz in range(4)], axis=1))
+        cst[rows, :] = jnp.transpose(right_stack(xs[k % 4])).astype(BF16)
 
     def fill_own(n, _):
         rows = pl.ds(pl.multiple_of(n * CHUNK, CHUNK), CHUNK)
@@ -172,7 +177,8 @@
 
         def distance(block):
             n, _, jb, pp = block
-            rows = pl.ds(pl.multiple_of(n * CHUNK + jb * TALL, TALL), TALL)
+            start = n * CHUNK + jb * TALL
+            rows = pl.ds(start if isinstance(n, int) else pl.multiple_of(start, TALL), TALL)
             return dot_nn(cst[rows, :], pst[:, pp * 256 : (pp + 1) * 256])
 
         ready = [distance(block) for block in blocks[:AHEAD]]
@@ -187,24 +193,44 @@
                 dst[2 * pp + half_at, pl.ds(base + jb * TALL, TALL), :] = high[:, part]
                 dst[2 * pp + half_at, pl.ds(base + CHUNK + jb * TALL, TALL), :] = low[:, part]
 
-    def fill_edges(n, _):
-        fill(stored, [(n, pl.multiple_of(n * (2 * CHUNK), 2 * CHUNK))], {})
-        return 0
-
-    build(0, 0)
+    def fill_stored(first, count):
+        def turn(i, _):
+            n = first + i * GROUP
+            fill(stored, [(n + k, row_of(n + k)) for k in range(GROUP)], {})
+            return 0
+
+        def row_of(n):
+            return pl.multiple_of(n * (2 * CHUNK), 2 * CHUNK)
+
+        whole = count // GROUP
+        if whole:
+            lax.fori_loop(0, whole, turn, 0)
+        for n in range(first + whole * GROUP, first + count):
+            fill(stored, [(n, n * 2 * CHUNK)], {})
+
+    build(0)
     p8[:, 0:128] = jnp.zeros((8, 128), F32)
     p8[0:4, 0:128] = centred(cpos[gy, z])
     ost[...] = left_stack(p8[:, 0:128]).astype(BF16)
-    lax.fori_loop(0, EARLY, fill_own, 0)
-    lax.fori_loop(0, EARLY, fill_edges, 0)
-
+    lax.fori_loop(0, 2, fill_own, 0)
+    fill_stored(0, 2)
+
+    near = cpos.at[0 : NEAR - 1]
+    pltpu.make_async_copy(near, near, rsem.at[1]).wait()
+    for k in range(1, NEAR):
+        build(k)
+    lax.fori_loop(2, 2 * NEAR, fill_own, 0, unroll=4)
+    fill_stored(2, EARLY - 2)
+
+    far = cpos.at[0 : N_GY - NEAR]
+    pltpu.make_async_copy(far, far, rsem.at[7]).wait()
+    for k in range(NEAR, N_GY):
+        build(k)
+    lax.fori_loop(2 * NEAR, NCHUNK, fill_own, 0, unroll=2)
     fifteen = cpos.at[0 : N_GY - 1]
-    pltpu.make_async_copy(fifteen, fifteen, rsem.at[1]).wait()
-    lax.fori_loop(1, N_GY, build, 0)
-    lax.fori_loop(EARLY, NCHUNK, fill_own, 0, unroll=2)
     others = cdis.at[0 : N_GY - 1]
     pltpu.make_async_copy(others, others, rsem.at[6]).wait()
-    order = [(lax.rem(gy + k, N_GY), zz) for k in range(N_GY) for zz in range(4)]
+    order = [(line, zz) for line in lines for zz in range(4)]
     d_ref[...] = jnp.concatenate([cdis[line, zz] for line, zz in order], axis=1)
 
     def set_search(search):
@@ -247,7 +273,7 @@
     set_search(d_ref[...])
     g1[me] = apply_own()
     spread(g1, 2)
-    lax.fori_loop(EARLY, EARLY + FIRST, fill_edges, 0)
+    fill_stored(EARLY, FIRST)
     arrive(g1, 2)
     d = d_ref[...]
     rr0 = total(d * d)
@@ -263,7 +289,7 @@
     set_search(search)
     g2[me] = apply_own()
     spread(g2, 3)
-    lax.fori_loop(EARLY + FIRST, STORED, fill_edges, 0)
+    fill_stored(EARLY + FIRST, FIRST)
     arrive(g2, 3)
     search = s_ref[...]
     applied = collected(g2) + SHIFT * search
@@ -287,15 +313,21 @@
 
     lane4 = lax.broadcasted_iota(jnp.int32, (4, 128), 1) < S
 
+    def at_chunk(n):
+        return n * 2 * CHUNK if isinstance(n, int) else pl.multiple_of(n * (2 * CHUNK), 2 * CHUNK)
+
     def contract(src, n, base, pp):
-        lhs = sp[:, pl.ds(pl.multiple_of(n * (2 * CHUNK), 2 * CHUNK), 2 * CHUNK)]
+        lhs = sp[:, pl.ds(at_chunk(n), 2 * CHUNK)]
         rows = pl.ds(base, 2 * CHUNK)
         cols = slice(pp * 256, (pp + 1) * 256)
         rhs = jnp.concatenate([src[2 * pp, rows, :], src[2 * pp + 1, rows, :]], axis=1)
         acc[:, cols] += dot_nn(lhs, rhs)
 
     def held(n, pp):
-        contract(stored, n, pl.multiple_of(n * (2 * CHUNK), 2 * CHUNK), pp)
+        contract(stored, n, at_chunk(n), pp)
+
+    turns = (NCHUNK - STORED) // 2
+    per = STORED // turns
 
     def fused(i, _):
         now = STORED + 2 * i
@@ -309,19 +341,18 @@
                     functools.partial(contract, fresh, now - 2 + c, c * 2 * CHUNK, pp)
                 )
         places = [at for at in range(blocks) if at % (blocks // 2) >= across]
-        pieces = [(n, pp) for n in range(PER) for pp in range(across)]
+        pieces = [(n, pp) for n in range(per) for pp in range(across)]
         for k, (n, pp) in enumerate(pieces):
             at = places[k * len(places) // len(pieces)]
-            extras.setdefault(at, []).append(functools.partial(held, PER * i + n, pp))
+            extras.setdefault(at, []).append(functools.partial(held, per * i + n, pp))
         fill(fresh, [(now, 0), (now + 1, 2 * CHUNK)], extras)
         return 0
 
-    turns = (NCHUNK - STORED) // 2
     lax.fori_loop(0, turns, fused, 0)
     for pp in range(POINTS // 256):
         for c in range(2):
             contract(fresh, NCHUNK - 2 + c, c * 2 * CHUNK, pp)
-        for n in range(PER * turns, STORED):
+        for n in range(per * turns, STORED):
             held(n, pp)
 
     for b in range(POINTS // 128):
@@ -346,9 +377,10 @@
         ).start()
 
     arrive(g3, 4)
-    summed = g3[0]
-    for q in range(1, CHIPS):
-        summed = summed + g3[q]
+    tiles = [g3[q] for q in range(CHIPS)]
+    while len(tiles) > 1:
+        tiles = [a + b for a, b in zip(tiles[::2], tiles[1::2])]
+    summed = tiles[0]
     step = ratio(rr2, total(summed))
     result = x_ref[:, mine] + step * s_ref[:, mine]
     result = jnp.where(core == 0, result, pltpu.roll(result, S, axis=1))
@@ -373,7 +405,7 @@
     pltpu.make_async_copy(box, box, ssem.at[5]).wait()
 
 
-WIDTH = 512
+WIDTH = 1024
 
 
 def blend_kernel(table_ref, count_ref, tile_ref, coef_ref, out_ref, copy_ref, st, lhs):
@@ -457,7 +489,7 @@
             pltpu.VMEM((16, POINTS), F32),
             pltpu.VMEM((16, NC), F32),
             pltpu.VMEM((16, 2 * NC), BF16),
-            pltpu.VMEM((8, 512), F32),
+            pltpu.VMEM((4, 8, 512), F32),
             pltpu.VMEM((4, NC), F32),
             pltpu.VMEM((4, NC), F32),
             pltpu.VMEM((4, NC), F32),
@@ -466,8 +498,8 @@
             pltpu.VMEM((N_GY, CAP, 4, 128), F32),
             pltpu.VMEM((N_GY, CAP, 4, 128), F32),
             pltpu.VMEM((8, POINTS), F32),
-            pltpu.SemaphoreType.DMA((7,)),
-            pltpu.SemaphoreType.DMA((7,)),
+            pltpu.SemaphoreType.DMA((8,)),
+            pltpu.SemaphoreType.DMA((8,)),
         ],
         compiler_params=pltpu.CompilerParams(
             collective_id=0, has_side_effects=True, vmem_limit_bytes=60 * 1024 * 1024

time: 62.4 us -> 57.8 us (0.926)
  Pallas kernels: 60.9 us -> 56.3 us
    pallas_call x1, Pallas kernels: 52.4 us -> 49.2 us  [shards(): pl.pallas_call(motion_kernel, out_shape=(jax.ShapeDtypeStruct((3, S), F32...]
    pallas_call x1, Pallas kernels: 8.52 us -> 7.06 us  [shards(): pl.pallas_call(blend_kernel, grid=(S * S // WIDTH,), out_shape=(jax.Shape...]
where the time goes in v3:
time: 57.8 us; the launch traced here: 57.6 us
  Pallas kernels  56.3 us (97%)
  between operations  1.29 us (2%)
    pallas_call x1, Pallas kernels, shards(): pl.pallas_call(motion_kernel, out_shape=(jax.ShapeDtypeStruct((3, S), F32...  49.2 us
    pallas_call x1, Pallas kernels, shards(): pl.pallas_call(blend_kernel, grid=(S * S // WIDTH,), out_shape=(jax.Shape...  7.06 us

profile of v3, /device:TPU:0, one launch (start us, length us, event | category | flops | bytes accessed | tf_op | source)
XLA Modules:
  0.0 57.6 jit_solution(1232321040906093250)
XLA Ops:
  1.3 49.2 %motion.1 = (f32[3,64]{1,0:T(4,128)}, f32[48,4,128]{2,1,0:T(4,128)}) custom-call(f32[3,64]{1,0:T(4,128)} %cen_ref.1, f32[3,64]{1,0:T(4,128)} %dis_ref.1, f32[3,1024]{1,0:T(4,128)} %pts_ref.1, s32[3,1,16]{2,1,0:T(1,128)} %bitcast.1), custom_call_target="tpu_custom_call" | custom-call | tf_op jit(solution)/shard_map/motion/pallas_call | solution.py:468
  50.5 7.1 %blend.1 = (f32[4,3,64,4096]{3,2,1,0:T(8,128)}, f32[3,64]{1,0:T(4,128)}) custom-call(s32[4,12]{1,0:T(4,128)} %table_ref.1, s32[1]{0:T(128)S(6)} %copy.8.count_ref, f32[48,4,128]{2,1,0:T(4,128)} %get-tuple-element.6.tile_ref, f32[3,64]{1,0:T(4,128)} %get-tuple-element.7.coef_ref), custom_call_target="tpu_custom_call" | custom-call | tf_op jit(solution)/shard_map/blend/pallas_call | solution.py:509

commit v4 on v3

--- a/solution.py
+++ b/solution.py
@@ -76,7 +76,7 @@
 
 EARLY = 6
 FIRST = 10
-GROUP = 2
+GROUP = 5
 STORED = EARLY + 2 * FIRST
 TALL = 64
 AHEAD = 2
@@ -362,18 +362,18 @@
         motion[2 * b] = jnp.where(lane4, first, pltpu.roll(second, S, axis=1))
         motion[2 * b + 1] = jnp.where(lane4, pltpu.roll(first, S, axis=1), second)
 
-    for k in range(N_GY):
-        to = lax.rem(gy + k, N_GY)
+    for k in reversed(range(N_GY)):
+        to = lines[k]
         for c in range(CAP):
             tile = motion[jnp.maximum(list_ref[c, 0, to], 0)]
             if k == 0:
                 inbox[gy, c] = tile
             else:
                 outbox[k, c] = tile
-    for k in range(1, N_GY):
+    for k in reversed(range(1, N_GY)):
         pltpu.make_async_remote_copy(
             src_ref=outbox.at[k], dst_ref=inbox.at[gy], send_sem=ssem.at[5], recv_sem=rsem.at[5],
-            device_id=(gx, lax.rem(gy + k, N_GY)), device_id_type=MESH,
+            device_id=(gx, lines[k]), device_id_type=MESH,
         ).start()
 
     arrive(g3, 4)

time: 57.8 us -> 57.4 us (level)
  no operation moved by 1% of the time
where the time goes in v4:
time: 57.4 us; the launch traced here: 57.2 us
  Pallas kernels  55.9 us (97%)
  between operations  1.29 us (2%)
    pallas_call x1, Pallas kernels, shards(): pl.pallas_call(motion_kernel, out_shape=(jax.ShapeDtypeStruct((3, S), F32...  48.8 us
    pallas_call x1, Pallas kernels, shards(): pl.pallas_call(blend_kernel, grid=(S * S // WIDTH,), out_shape=(jax.Shape...  7.07 us

profile of v4, /device:TPU:0, one launch (start us, length us, event | category | flops | bytes accessed | tf_op | source)
XLA Modules:
  0.0 57.2 jit_solution(9338466589681002026)
XLA Ops:
  1.3 48.8 %motion.1 = (f32[3,64]{1,0:T(4,128)}, f32[48,4,128]{2,1,0:T(4,128)}) custom-call(f32[3,64]{1,0:T(4,128)} %cen_ref.1, f32[3,64]{1,0:T(4,128)} %dis_ref.1, f32[3,1024]{1,0:T(4,128)} %pts_ref.1, s32[3,1,16]{2,1,0:T(1,128)} %bitcast.1), custom_call_target="tpu_custom_call" | custom-call | tf_op jit(solution)/shard_map/motion/pallas_call | solution.py:468
  50.1 7.1 %blend.1 = (f32[4,3,64,4096]{3,2,1,0:T(8,128)}, f32[3,64]{1,0:T(4,128)}) custom-call(s32[4,12]{1,0:T(4,128)} %table_ref.1, s32[1]{0:T(128)S(6)} %copy.8.count_ref, f32[48,4,128]{2,1,0:T(4,128)} %get-tuple-element.6.tile_ref, f32[3,64]{1,0:T(4,128)} %get-tuple-element.7.coef_ref), custom_call_target="tpu_custom_call" | custom-call | tf_op jit(solution)/shard_map/blend/pallas_call | solution.py:509
